TPU v7x, 32 devices: a whole 2x2x4 slice. The times are simulated.
32 devices in a mesh: seq: 8 (over z, y), head: 4 (over x, core).
Axes of the slice: x: 2, y: 2, z: 4, core: 2. Of those that a mesh axis runs over, the one named last changes fastest.
Arguments:
- queries: bfloat16 [4096, 2048], P('seq', 'head'), may hold values from -8 to 8
- keys: bfloat16 [4096, 1024], P('seq', 'head'), may hold values from -8 to 8
- values: bfloat16 [4096, 1024], P('seq', 'head'), may hold values from -6 to 6
- output_gradient: bfloat16 [4096, 2048], P('seq', 'head'), may hold values from -6 to 6
- key_exponents: int32 [32, 8], P('seq', 'head'), may hold values from -1 to 1
- value_exponents: int32 [32, 8], P('seq', 'head'), may hold values from -1 to 1
- key_matrix: bfloat16 [5376, 1024], P(None, 'head'), may hold values from -0.1875 to 0.1875
- value_matrix: bfloat16 [5376, 1024], P(None, 'head'), may hold values from -0.1875 to 0.1875
Outputs:
- query_grad: bfloat16 [4096, 2048], P('seq', 'head')
- input_grad: bfloat16 [5376, 4096], P('head', 'seq')
All inputs are finite; a program needn't handle non-finite values.
Results may differ from a plain program's by a relative error of at most 0.015.
Values may be sent and summed in bfloat16 or wider, within the bound.
A program may use at most 64 MiB of HBM per device.

v0:
```python
import jax
import jax.numpy as jnp
from jax import lax
from jax.sharding import PartitionSpec as P

HEAD_SIZE = 128
QUERY_SCALE = 168
ATTEND_WINDOW = 1024
SCALE_BLOCK = 128


def passed_along(value, axis, steps):
    count = lax.axis_size(axis)
    first, last = (max(0, -steps), min(count, count - steps))
    return lax.ppermute(value, axis, [(source, source + steps) for source in range(first, last)])


def power_of_two(exponents):
    return jnp.where(exponents > 0, 2.0, jnp.where(exponents < 0, 0.5, 1.0)).astype(jnp.float32)


def dequantize(stored, exponents):
    row_count = stored.shape[0]
    head_count = exponents.shape[1]
    factor = jnp.repeat(power_of_two(exponents), SCALE_BLOCK, axis=0)
    shaped = (
        stored.astype(jnp.float32).reshape(row_count, head_count, HEAD_SIZE) * factor[:, :, None]
    )
    return (shaped.reshape(row_count, head_count * HEAD_SIZE).astype(jnp.bfloat16), factor)


def window_means(raw_window, first_target, target_count, first_source):
    target_at = first_target + jnp.arange(target_count, dtype=jnp.int32)
    source_at = first_source + jnp.arange(raw_window.shape[0], dtype=jnp.int32)
    distance = target_at[:, None] - source_at[None, :]
    band = ((distance >= 0) & (distance < ATTEND_WINDOW)).astype(jnp.bfloat16)
    sums = jnp.dot(band, raw_window, preferred_element_type=jnp.float32)
    counts = jnp.clip(target_at + 1, 1, ATTEND_WINDOW).astype(jnp.float32)
    return sums / counts[:, None]


def attend(query_rows, grad_rows, smooth_window, value_window, first_key, first_query):
    token_count = query_rows.shape[0]
    key_count = smooth_window.shape[0]
    key_value_heads = smooth_window.shape[1] // HEAD_SIZE
    group_width = query_rows.shape[1] // (key_value_heads * HEAD_SIZE)
    score_scale = QUERY_SCALE ** (-0.5)
    query_at = first_query + jnp.arange(token_count, dtype=jnp.int32)
    key_at = first_key + jnp.arange(key_count, dtype=jnp.int32)
    distance = query_at[:, None] - key_at[None, :]
    allowed = (distance >= 0) & (distance < ATTEND_WINDOW) & (key_at[None, :] >= 0)
    query_head_count = query_rows.reshape(
        token_count, key_value_heads, group_width, HEAD_SIZE
    ).transpose(1, 2, 0, 3)
    gradient_heads = grad_rows.reshape(
        token_count, key_value_heads, group_width, HEAD_SIZE
    ).transpose(1, 2, 0, 3)
    key_heads = smooth_window.reshape(key_count, key_value_heads, HEAD_SIZE).transpose(1, 0, 2)
    value_heads = value_window.reshape(key_count, key_value_heads, HEAD_SIZE).transpose(1, 0, 2)

    def one_head(operands):
        head_queries, head_grads, head_keys, head_values = operands
        scores = (
            jnp.einsum("gqd,kd->gqk", head_queries, head_keys, preferred_element_type=jnp.float32)
            * score_scale
        )
        scores = jnp.where(allowed, scores, -jnp.inf)
        highest = jnp.max(scores, axis=-1, keepdims=True)
        weights = jnp.exp(scores - highest)
        shares = weights / jnp.sum(weights, axis=-1, keepdims=True)
        rounded = shares.astype(jnp.bfloat16)
        attended = jnp.einsum(
            "gqk,kd->gqd", rounded, head_values, preferred_element_type=jnp.float32
        )
        row_dot = jnp.sum(attended * head_grads.astype(jnp.float32), axis=-1, keepdims=True)
        share_grad = jnp.einsum(
            "gqd,kd->gqk", head_grads, head_values, preferred_element_type=jnp.float32
        )
        score_grad = (shares * (share_grad - row_dot)).astype(jnp.bfloat16)
        query_part = (
            score_scale
            * jnp.einsum("gqk,kd->qgd", score_grad, head_keys, preferred_element_type=jnp.float32)
        ).astype(jnp.bfloat16)
        key_part = score_scale * jnp.einsum(
            "gqk,gqd->kd", score_grad, head_queries, preferred_element_type=jnp.float32
        )
        value_part = jnp.einsum(
            "gqk,gqd->kd", rounded, head_grads, preferred_element_type=jnp.float32
        )
        return (query_part, key_part, value_part)

    query_part, key_part, value_part = lax.map(
        one_head, (query_head_count, gradient_heads, key_heads, value_heads)
    )
    query_grad = query_part.transpose(1, 0, 2, 3).reshape(
        token_count, key_value_heads * group_width * HEAD_SIZE
    )
    key_grad = key_part.transpose(1, 0, 2).reshape(key_count, key_value_heads * HEAD_SIZE)
    value_grad = value_part.transpose(1, 0, 2).reshape(key_count, key_value_heads * HEAD_SIZE)
    return (query_grad, key_grad, value_grad)


def local(
    queries, keys, values, output_gradient, key_exponents, value_exponents, key_matrix, value_matrix
):
    token_count = queries.shape[0]
    reach = ATTEND_WINDOW // token_count
    first_query = lax.axis_index("seq") * token_count
    first_key = first_query - reach * token_count
    exact_keys, key_multiplier = dequantize(keys, key_exponents)
    exact_values, value_multiplier = dequantize(values, value_exponents)
    raw_pieces = [passed_along(exact_keys, "seq", distance) for distance in range(reach, 0, -1)]
    raw_window = jnp.concatenate(raw_pieces + [exact_keys], 0)
    means = window_means(raw_window, first_query, token_count, first_key)
    smooth_own = (exact_keys.astype(jnp.float32) - means).astype(jnp.bfloat16)
    smooth_pieces = []
    value_pieces = []
    for distance in range(reach, 0, -1):
        smooth_piece, value_piece = passed_along((smooth_own, exact_values), "seq", distance)
        smooth_pieces.append(smooth_piece)
        value_pieces.append(value_piece)
    smooth_window = jnp.concatenate(smooth_pieces + [smooth_own], 0)
    value_window = jnp.concatenate(value_pieces + [exact_values], 0)
    query_grad, key_window_grad, value_window_grad = attend(
        queries, output_gradient, smooth_window, value_window, first_key, first_query
    )

    def slot_rows(array, distance):
        begin_row = (reach - distance) * token_count
        return array[begin_row : begin_row + token_count]

    key_grad = slot_rows(key_window_grad, 0)
    value_grad = slot_rows(value_window_grad, 0)
    for distance in range(1, reach + 1):
        moved_key, moved_value = (
            passed_along(
                slot_rows(key_window_grad, distance).astype(jnp.bfloat16), "seq", -distance
            ).astype(jnp.float32),
            passed_along(
                slot_rows(value_window_grad, distance).astype(jnp.bfloat16), "seq", -distance
            ).astype(jnp.float32),
        )
        key_grad = key_grad + moved_key
        value_grad = value_grad + moved_value
    scaled_keys = (key_grad * jnp.repeat(key_multiplier, HEAD_SIZE, axis=1)).astype(jnp.bfloat16)
    scaled_values = (value_grad * jnp.repeat(value_multiplier, HEAD_SIZE, axis=1)).astype(
        jnp.bfloat16
    )
    key_columns = scaled_keys.T
    value_columns = scaled_values.T
    input_grad = lax.psum_scatter(
        (
            jnp.dot(key_matrix, key_columns, preferred_element_type=jnp.float32)
            + jnp.dot(value_matrix, value_columns, preferred_element_type=jnp.float32)
        ).astype(jnp.bfloat16),
        "head",
        scatter_dimension=0,
        tiled=True,
    )
    return (query_grad, input_grad)


def solution(mesh):
    in_specs = (
        P("seq", "head"),
        P("seq", "head"),
        P("seq", "head"),
        P("seq", "head"),
        P("seq", "head"),
        P("seq", "head"),
        P(None, "head"),
        P(None, "head"),
    )
    out_specs = (P("seq", "head"), P("head", "seq"))
    return jax.shard_map(local, mesh=mesh, in_specs=in_specs, out_specs=out_specs, check_vma=False)
```

profile of v0, /device:TPU:0, one launch (start us, length us, event | category | flops | bytes accessed | tf_op | source)
XLA Modules:
  0.0 194.8 jit_solution(5987780303244949135)
XLA Ops:
  9.3 5.6 %collective-permute-start.5 = (bf16[512,256]{0,1:T(8,128)(2,1)S(1)}, bf16[512,256]{0,1:T(8,128)(2,1)}, u32[]{:S(2)}, u32[]{:S(2)}) collective-permute-start(bf16[512,256]{0,1:T(8,128)(2,1)S(1)} %fusion.76), channel_id=1, source_target_pairs={{0,4},{4,8},{8,12},{12,16},{16,20},{20,24},{24,28},{1,5},{5,9},{9,... | collective-permute-start | bytes 786440 | tf_op jit(solution)/shard_map/ppermute | solution.py:15
  14.9 3.5 %collective-permute-start.4 = (bf16[512,256]{0,1:T(8,128)(2,1)S(1)}, bf16[512,256]{0,1:T(8,128)(2,1)}, u32[]{:S(2)}, u32[]{:S(2)}) collective-permute-start(bf16[512,256]{0,1:T(8,128)(2,1)S(1)} %fusion.76), channel_id=1, source_target_pairs={{0,8},{4,12},{8,16},{12,20},{16,24},{20,28},{1,9},{5,13},{9,17},{1... | collective-permute-start | bytes 786440 | tf_op jit(solution)/shard_map/ppermute | solution.py:15
  20.6 1.7 fusion.78
  22.3 4.1 %collective-permute-start.1 = (bf16[512,256]{1,0:T(8,128)(2,1)}, bf16[512,256]{1,0:T(8,128)(2,1)}, u32[]{:S(2)}, u32[]{:S(2)}) collective-permute-start(bf16[512,256]{1,0:T(8,128)(2,1)} %fusion.78), channel_id=1, source_target_pairs={{0,4},{4,8},{8,12},{12,16},{16,20},{20,24},{24,28},{1,5},{5,9},{9,... | collective-permute-start | bytes 786440 | tf_op jit(solution)/shard_map/ppermute | solution.py:15
  26.5 2.8 %collective-permute-start = (bf16[512,256]{1,0:T(8,128)(2,1)}, bf16[512,256]{1,0:T(8,128)(2,1)}, u32[]{:S(2)}, u32[]{:S(2)}) collective-permute-start(bf16[512,256]{1,0:T(8,128)(2,1)} %fusion.78), channel_id=1, source_target_pairs={{0,8},{4,12},{8,16},{12,20},{16,24},{20,28},{1,9},{5,13},{9,17},{1... | collective-permute-start | bytes 786440 | tf_op jit(solution)/shard_map/ppermute | solution.py:15
  29.3 1.8 collective-permute-done.1
  31.0 2.5 %collective-permute-done = bf16[512,256]{1,0:T(8,128)(2,1)} collective-permute-done((bf16[512,256]{1,0:T(8,128)(2,1)}, bf16[512,256]{1,0:T(8,128)(2,1)}, u32[]{:S(2)}, u32[]{:S(2)}) %collective-permute-start) | collective-permute-done | bytes 262176 | tf_op jit(solution)/shard_map/ppermute | solution.py:15
  33.6 2.8 %fusion.68 = bf16[512,256]{1,0:T(8,128)(2,1)} fusion(s32[1536]{0:T(1024)S(1)} %iota_add_fusion, s32[512]{0:T(512)S(1)} %iota_add_fusion.1, bf16[512,256]{1,0:T(8,128)(2,1)} %fusion.78, bf16[512,256]{1,0:T(8,128)(2,1)} %collective-permute-done.1, bf16[512,256]{1,0:T(8,128)(2,1)} %collective-permute-done, f32[512]{0:T(512)S(1)} %clamp_convert_fusion), kind=kOutput, calls=%fused_computation.68 | convolution fusion | flops 408682496 | bytes 1058816 | tf_op jit(solution)/shard_map/dot_general | solution.py:37
  36.4 7.3 %collective-permute-start.3 = (bf16[512,256]{1,0:T(8,128)(2,1)}, bf16[512,256]{1,0:T(8,128)(2,1)}, u32[]{:S(2)}, u32[]{:S(2)}) collective-permute-start(bf16[512,256]{1,0:T(8,128)(2,1)} %fusion.68), channel_id=1, source_target_pairs={{0,4},{4,8},{8,12},{12,16},{16,20},{20,24},{24,28},{1,5},{5,9},{9,... | collective-permute-start | bytes 786440 | tf_op jit(solution)/shard_map/ppermute | solution.py:15
  43.7 4.4 %collective-permute-start.2 = (bf16[512,256]{1,0:T(8,128)(2,1)}, bf16[512,256]{1,0:T(8,128)(2,1)}, u32[]{:S(2)}, u32[]{:S(2)}) collective-permute-start(bf16[512,256]{1,0:T(8,128)(2,1)} %fusion.68), channel_id=1, source_target_pairs={{0,8},{4,12},{8,16},{12,20},{16,24},{20,28},{1,9},{5,13},{9,17},{1... | collective-permute-start | bytes 786440 | tf_op jit(solution)/shard_map/ppermute | solution.py:15
  50.4 2.0 %pad_maximum_fusion = bf16[1536,256]{0,1:T(8,128)(2,1)} fusion(bf16[512,256]{0,1:T(8,128)(2,1)S(1)} %fusion.76, bf16[512,256]{0,1:T(8,128)(2,1)} %collective-permute-done.5, bf16[512,256]{0,1:T(8,128)(2,1)} %collective-permute-done.4), kind=kLoop, calls=%fused_computation.76 | loop fusion | flops 2359296 | bytes 1572864 | tf_op jit(solution)/shard_map/concatenate | solution.py:123
  52.3 2.1 %bitcast_bitcast_fusion = bf16[2,1536,128]{2,1,0:T(8,128)(2,1)} fusion(bf16[512,256]{1,0:T(8,128)(2,1)} %fusion.68, bf16[512,256]{1,0:T(8,128)(2,1)} %collective-permute-done.3, bf16[512,256]{1,0:T(8,128)(2,1)} %collective-permute-done.2), kind=kLoop, calls=%fused_computation.69 | loop fusion | flops 2359296 | bytes 1572864 | tf_op jit(solution)/shard_map/transpose | solution.py:58
  54.5 40.1 %while.15 = (s32[]{:T(128)}, bf16[2,512,2,128]{1,3,2,0:T(8,128)(2,1)}, f32[2,1536,128]{2,1,0:T(8,128)}, f32[2,1536,128]{1,2,0:T(8,128)}, bf16[2,1536,128]{2,1,0:...) while((s32[]{:T(128)}, ...), condition=%wide.region_4.5_spmd.clone, body=%wide.region_0.4_spmd.clone.sunk | while | flops 2436432384 | bytes 113294400 | solution.py:92
  57.0 6.2 %fusion.132 = (f32[2,512]{1,0:T(2,128)S(1)}, f32[2,512,1536]{2,1,0:T(8,128)}) fusion(pred[512,1536]{1,0:T(8,128)(4,1)S(1)} %fusion.131, bf16[2,1536,128]{2,1,0:T(8,128)(2,1)} %get-tuple-element.236, s32[]{:T(128)S(6)} %copy.103, bf16[2,2,512,128]{2,3,1,0:T(8,128)(2,1)} %get-tuple-element.237), kind=kOutput, calls=%fused_computation.109.clone.1 | convolution fusion | flops 408946176 | bytes 7738368 | tf_op jit(solution)/shard_map/while/body/eval_jaxpr/sub | solution.py:69
  63.2 3.8 %fusion.133 = bf16[2,512,1536]{2,1,0:T(8,128)(2,1)S(1)} fusion(f32[2,512,1536]{2,1,0:T(8,128)} %get-tuple-element.206, f32[2,512]{1,0:T(2,128)S(1)} %get-tuple-element.207), kind=kLoop, calls=%fused_computation.14.clone.1 | loop fusion | flops 3145728 | bytes 9441280 | tf_op jit(solution)/shard_map/while/body/eval_jaxpr/convert_element_type | solution.py:71
  77.0 6.2 %fusion.132 = (f32[2,512]{1,0:T(2,128)S(1)}, f32[2,512,1536]{2,1,0:T(8,128)}) fusion(pred[512,1536]{1,0:T(8,128)(4,1)S(1)} %fusion.131, bf16[2,1536,128]{2,1,0:T(8,128)(2,1)} %get-tuple-element.236, s32[]{:T(128)S(6)} %copy.103, bf16[2,2,512,128]{2,3,1,0:T(8,128)(2,1)} %get-tuple-element.237), kind=kOutput, calls=%fused_computation.109.clone.1 | convolution fusion | flops 408946176 | bytes 7738368 | tf_op jit(solution)/shard_map/while/body/eval_jaxpr/sub | solution.py:69
  83.2 3.8 %fusion.133 = bf16[2,512,1536]{2,1,0:T(8,128)(2,1)S(1)} fusion(f32[2,512,1536]{2,1,0:T(8,128)} %get-tuple-element.206, f32[2,512]{1,0:T(2,128)S(1)} %get-tuple-element.207), kind=kLoop, calls=%fused_computation.14.clone.1 | loop fusion | flops 3145728 | bytes 9441280 | tf_op jit(solution)/shard_map/while/body/eval_jaxpr/convert_element_type | solution.py:71
  94.5 1.6 bitcast_convert_fusion
  102.9 4.7 %collective-permute-done.9 = bf16[512,256]{0,1:T(8,128)(2,1)S(1)} collective-permute-done((bf16[512,256]{0,1:T(8,128)(2,1)S(1)}, bf16[512,256]{0,1:T(8,128)(2,1)S(1)}, u32[]{:S(2)}, u32[]{:S(2)}) %collective-permute-start.9) | collective-permute-done | bytes 262176 | tf_op jit(solution)/shard_map/ppermute | solution.py:15
  107.8 1.7 fusion.92
  109.5 9.4 %collective-permute-done.7 = bf16[512,256]{1,0:T(8,128)(2,1)S(1)} collective-permute-done((bf16[512,256]{1,0:T(8,128)(2,1)S(1)}, bf16[512,256]{1,0:T(8,128)(2,1)S(1)}, u32[]{:S(2)}, u32[]{:S(2)}) %collective-permute-start.7) | collective-permute-done | bytes 262176 | tf_op jit(solution)/shard_map/ppermute | solution.py:15
  118.9 4.1 %fusion.54 = bf16[5376,512]{0,1:T(8,128)(2,1)} fusion(f32[512,5376]{1,0:T(8,128)S(1)} %fusion.92, bf16[5376,256]{1,0:T(8,128)(2,1)S(1)} %copy-done.14, bf16[512,256]{1,0:T(8,128)(2,1)S(1)} %collective-permute-done.7, bf16[512,256]{1,0:T(8,128)(2,1)S(1)} %collective-permute-done.6, f32[64,8,2,128]{3,2,1,0:T(2,128)S(1)} %bitcast.192, ...), kind=kOutput, calls=%fused_computation.57 | convolution fusion | flops 1415577600 | bytes 20840448 | tf_op jit(solution)/shard_map/dot_general | solution.py:153
  123.0 8.3 %copy.69 = bf16[5376,512]{1,0:T(8,128)(2,1)} copy(bf16[5376,512]{0,1:T(8,128)(2,1)} %fusion.54) | data formatting | bytes 11010048
  133.4 54.6 %reduce-scatter.4.cloned.1.call-done = bf16[1344,512]{1,0:T(8,128)(2,1)} async-done(((bf16[5376,512]{1,0:T(8,128)(2,1)}), bf16[1344,512]{1,0:T(8,128)(2,1)}) %reduce-scatter.4.cloned.1.call-update) | async-done | bytes 1376272
  (132 shorter events, 35.4 us)
Async XLA Ops:
  7.2 100.6 %copy-start = (bf16[5376,256]{1,0:T(8,128)(2,1)S(1)}, bf16[5376,256]{1,0:T(8,128)(2,1)}, u32[]{:S(2)}) copy-start(bf16[5376,256]{1,0:T(8,128)(2,1)} %param.17) | copy-start | bytes 8257540
  7.2 180.8 %reduce-scatter.4.cloned.1.call-start = ((), (), s32[]{:S(2)}) async-start(), calls=%async_computation.1 | async-start | bytes 6881280
  8.1 21.1 %copy-start.22 = (f32[1,2,4,128]{3,1,2,0:T(2,128)}, f32[1,2,4,128]{3,1,2,0:T(2,128)S(1)}, u32[]{:S(2)}) copy-start(f32[1,2,4,128]{3,1,2,0:T(2,128)S(1)} %copy.93) | copy-start | bytes 12292
  9.3 41.1 %collective-permute-start.5 = (bf16[512,256]{0,1:T(8,128)(2,1)S(1)}, bf16[512,256]{0,1:T(8,128)(2,1)}, u32[]{:S(2)}, u32[]{:S(2)}) collective-permute-start(bf16[512,256]{0,1:T(8,128)(2,1)S(1)} %fusion.76), channel_id=1, source_target_pairs={{0,4},{4,8},{8,12},{12,16},{16,20},{20,24},{24,28},{1,5},{5,9},{9,... | collective-permute-start | bytes 786440 | tf_op jit(solution)/shard_map/ppermute | solution.py:15
  14.9 35.5 %collective-permute-start.4 = (bf16[512,256]{0,1:T(8,128)(2,1)S(1)}, bf16[512,256]{0,1:T(8,128)(2,1)}, u32[]{:S(2)}, u32[]{:S(2)}) collective-permute-start(bf16[512,256]{0,1:T(8,128)(2,1)S(1)} %fusion.76), channel_id=1, source_target_pairs={{0,8},{4,12},{8,16},{12,20},{16,24},{20,28},{1,9},{5,13},{9,17},{1... | collective-permute-start | bytes 786440 | tf_op jit(solution)/shard_map/ppermute | solution.py:15
  22.3 8.7 %collective-permute-start.1 = (bf16[512,256]{1,0:T(8,128)(2,1)}, bf16[512,256]{1,0:T(8,128)(2,1)}, u32[]{:S(2)}, u32[]{:S(2)}) collective-permute-start(bf16[512,256]{1,0:T(8,128)(2,1)} %fusion.78), channel_id=1, source_target_pairs={{0,4},{4,8},{8,12},{12,16},{16,20},{20,24},{24,28},{1,5},{5,9},{9,... | collective-permute-start | bytes 786440 | tf_op jit(solution)/shard_map/ppermute | solution.py:15
  26.5 7.1 %collective-permute-start = (bf16[512,256]{1,0:T(8,128)(2,1)}, bf16[512,256]{1,0:T(8,128)(2,1)}, u32[]{:S(2)}, u32[]{:S(2)}) collective-permute-start(bf16[512,256]{1,0:T(8,128)(2,1)} %fusion.78), channel_id=1, source_target_pairs={{0,8},{4,12},{8,16},{12,20},{16,24},{20,28},{1,9},{5,13},{9,17},{1... | collective-permute-start | bytes 786440 | tf_op jit(solution)/shard_map/ppermute | solution.py:15
  29.3 18.8 %copy-start.16 = (bf16[512,512]{1,0:T(8,128)(2,1)S(1)}, bf16[512,512]{1,0:T(8,128)(2,1)}, u32[]{:S(2)}) copy-start(bf16[512,512]{1,0:T(8,128)(2,1)} %param.10) | copy-start | bytes 1572868
  36.4 15.9 %collective-permute-start.3 = (bf16[512,256]{1,0:T(8,128)(2,1)}, bf16[512,256]{1,0:T(8,128)(2,1)}, u32[]{:S(2)}, u32[]{:S(2)}) collective-permute-start(bf16[512,256]{1,0:T(8,128)(2,1)} %fusion.68), channel_id=1, source_target_pairs={{0,4},{4,8},{8,12},{12,16},{16,20},{20,24},{24,28},{1,5},{5,9},{9,... | collective-permute-start | bytes 786440 | tf_op jit(solution)/shard_map/ppermute | solution.py:15
  43.7 8.6 %collective-permute-start.2 = (bf16[512,256]{1,0:T(8,128)(2,1)}, bf16[512,256]{1,0:T(8,128)(2,1)}, u32[]{:S(2)}, u32[]{:S(2)}) collective-permute-start(bf16[512,256]{1,0:T(8,128)(2,1)} %fusion.68), channel_id=1, source_target_pairs={{0,8},{4,12},{8,16},{12,20},{16,24},{20,28},{1,9},{5,13},{9,17},{1... | collective-permute-start | bytes 786440 | tf_op jit(solution)/shard_map/ppermute | solution.py:15
  63.2 3.8 %copy-start.5 = (bf16[1,2,512,128]{3,2,1,0:T(8,128)(2,1)S(1)}, bf16[1,2,512,128]{3,2,1,0:T(8,128)(2,1)}, u32[]{:S(2)}) copy-start(bf16[1,2,512,128]{3,2,1,0:T(8,128)(2,1)} %copy.95) | copy-start | bytes 786436 | tf_op jit(solution)/shard_map/while
  63.2 3.8 %copy-start.15 = (bf16[2,1536,128]{1,2,0:T(8,128)(2,1)S(1)}, bf16[2,1536,128]{1,2,0:T(8,128)(2,1)}, u32[]{:S(2)}) copy-start(bf16[2,1536,128]{1,2,0:T(8,128)(2,1)} %get-tuple-element.239) | copy-start | bytes 2359300 | tf_op jit(solution)/shard_map/while
  63.2 4.9 %copy-start.1 = (f32[2,512,1536]{2,1,0:T(8,128)S(1)}, f32[2,512,1536]{2,1,0:T(8,128)}, u32[]{:S(2)}) copy-start(f32[2,512,1536]{2,1,0:T(8,128)} %get-tuple-element.206) | copy-start | bytes 18874372 | tf_op jit(solution)/shard_map/while
  83.2 3.8 %copy-start.5 = (bf16[1,2,512,128]{3,2,1,0:T(8,128)(2,1)S(1)}, bf16[1,2,512,128]{3,2,1,0:T(8,128)(2,1)}, u32[]{:S(2)}) copy-start(bf16[1,2,512,128]{3,2,1,0:T(8,128)(2,1)} %copy.95) | copy-start | bytes 786436 | tf_op jit(solution)/shard_map/while
  83.2 3.8 %copy-start.15 = (bf16[2,1536,128]{1,2,0:T(8,128)(2,1)S(1)}, bf16[2,1536,128]{1,2,0:T(8,128)(2,1)}, u32[]{:S(2)}) copy-start(bf16[2,1536,128]{1,2,0:T(8,128)(2,1)} %get-tuple-element.239) | copy-start | bytes 2359300 | tf_op jit(solution)/shard_map/while
  83.2 4.9 %copy-start.1 = (f32[2,512,1536]{2,1,0:T(8,128)S(1)}, f32[2,512,1536]{2,1,0:T(8,128)}, u32[]{:S(2)}) copy-start(f32[2,512,1536]{2,1,0:T(8,128)} %get-tuple-element.206) | copy-start | bytes 18874372 | tf_op jit(solution)/shard_map/while
  94.5 4.3 %copy-start.11 = (f32[2,1536,128]{2,1,0:T(8,128)S(1)}, f32[2,1536,128]{2,1,0:T(8,128)}, u32[]{:S(2)}) copy-start(f32[2,1536,128]{2,1,0:T(8,128)} %get-tuple-element.52) | copy-start | bytes 4718596
  96.1 11.5 %copy-start.23 = (f32[1,2,4,128]{3,1,2,0:T(2,128)S(1)}, f32[1,2,4,128]{3,1,2,0:T(2,128)}, u32[]{:S(2)}) copy-start(f32[1,2,4,128]{3,1,2,0:T(2,128)} %copy-done.22) | copy-start | bytes 12292
  96.2 11.5 %collective-permute-start.9 = (bf16[512,256]{0,1:T(8,128)(2,1)S(1)}, bf16[512,256]{0,1:T(8,128)(2,1)S(1)}, u32[]{:S(2)}, u32[]{:S(2)}) collective-permute-start(bf16[512,256]{0,1:T(8,128)(2,1)S(1)} %bitcast.201), channel_id=1, source_target_pairs={{8,0},{12,4},{16,8},{20,12},{24,16},{28,20},{9,1},{13,5},{17,9},{2... | collective-permute-start | bytes 786440 | tf_op jit(solution)/shard_map/ppermute | solution.py:15
  97.5 10.2 %collective-permute-start.8 = (bf16[512,256]{0,1:T(8,128)(2,1)S(1)}, bf16[512,256]{0,1:T(8,128)(2,1)S(1)}, u32[]{:S(2)}, u32[]{:S(2)}) collective-permute-start(bf16[512,256]{0,1:T(8,128)(2,1)S(1)} %bitcast.200), channel_id=1, source_target_pairs={{4,0},{8,4},{12,8},{16,12},{20,16},{24,20},{28,24},{5,1},{9,5},{13... | collective-permute-start | bytes 786440 | tf_op jit(solution)/shard_map/ppermute | solution.py:15
  100.2 18.8 %collective-permute-start.7 = (bf16[512,256]{1,0:T(8,128)(2,1)S(1)}, bf16[512,256]{1,0:T(8,128)(2,1)S(1)}, u32[]{:S(2)}, u32[]{:S(2)}) collective-permute-start(bf16[512,256]{1,0:T(8,128)(2,1)S(1)} %bitcast.199), channel_id=1, source_target_pairs={{8,0},{12,4},{16,8},{20,12},{24,16},{28,20},{9,1},{13,5},{17,9},{2... | collective-permute-start | bytes 786440 | tf_op jit(solution)/shard_map/ppermute | solution.py:15
  101.5 17.5 %collective-permute-start.6 = (bf16[512,256]{1,0:T(8,128)(2,1)S(1)}, bf16[512,256]{1,0:T(8,128)(2,1)S(1)}, u32[]{:S(2)}, u32[]{:S(2)}) collective-permute-start(bf16[512,256]{1,0:T(8,128)(2,1)S(1)} %bitcast.198), channel_id=1, source_target_pairs={{4,0},{8,4},{12,8},{16,12},{20,16},{24,20},{28,24},{5,1},{9,5},{13... | collective-permute-start | bytes 786440 | tf_op jit(solution)/shard_map/ppermute | solution.py:15
  107.8 11.1 %copy-start.8 = (f32[512,2,128]{2,1,0:T(2,128)S(1)}, f32[512,2,128]{2,1,0:T(2,128)}, u32[]{:S(2)}) copy-start(f32[512,2,128]{2,1,0:T(2,128)} %copy-done.7) | copy-start | bytes 1572868
  107.8 11.1 %copy-start.14 = (bf16[5376,256]{1,0:T(8,128)(2,1)S(1)}, bf16[5376,256]{1,0:T(8,128)(2,1)}, u32[]{:S(2)}) copy-start(bf16[5376,256]{1,0:T(8,128)(2,1)} %param.16) | copy-start | bytes 8257540
  (26 other events, 40.4 us)
Sparse Core Ops, SparseCore 0:
  131.5 56.4 reduce-scatter.3
where the time goes:
time: 196 us; the launch traced here: 195 us
  waiting for transfers between devices  73 us (37%)
  starting transfers between devices  33.1 us (17%)
  matrix products  31.3 us (16%)
  local copies, waits for them, and re-layouts  24.4 us (12%)
  other arithmetic  18.5 us (9%)
  between operations  14.3 us (7%)
    unnamed x2, waiting for transfers between devices  54.6 us
    ppermute x10, starting transfers between devices, passed_along(): lax.ppermute(value, axis, [(source, source + steps) for source in range(f...  33 us
    ppermute x10, waiting for transfers between devices, passed_along(): lax.ppermute(value, axis, [(source, source + steps) for source in range(f...  18.4 us
    unnamed x25, local copies, waits for them, and re-layouts  13.6 us
    sub x2, matrix products, one_head(): weights = jnp.exp(scores - highest)  12.4 us
    convert_element_type x2, other arithmetic, one_head(): rounded = shares.astype(jnp.bfloat16)  7.51 us
    while x60, local copies, waits for them, and re-layouts  6.08 us
    dot_general x1, matrix products, local(): jnp.dot(key_matrix, key_columns, preferred_element_type=jnp.float32)  4.1 us
  transfers between devices with their start and end apart: 11, of which 5 were waited for; matrix products, arithmetic and copies ran while one was open for 7% of the time, Pallas kernels for 0%

commit v1 on v0

v1 whole, which is shorter than its diff:
```python
import functools

import jax
import jax.numpy as jnp
from jax import lax
from jax.experimental import pallas as pl
from jax.experimental.pallas import tpu as pltpu
from jax.sharding import PartitionSpec as P

HEAD_SIZE = 128
QUERY_SCALE = 168
ATTEND_WINDOW = 1024
SCALE_BLOCK = 128
LOG2_E = 1.4426950408889634
MESH = pl.DeviceIdType.MESH
F32 = jnp.float32
BF16 = jnp.bfloat16


def power_of_two(exponent):
    return jnp.where(exponent > 0, 2.0, jnp.where(exponent < 0, 0.5, 1.0)).astype(F32)


def contract_last(a, b):
    return lax.dot_general(a, b, (((1,), (1,)), ((), ())), preferred_element_type=F32)


def partner(h, t):
    other, bit = h, 1
    while bit <= t:
        if t & bit:
            other = other + bit - 2 * bit * lax.rem(lax.div(h, bit), 2)
        bit *= 2
    return other


def kernel(
    n, nh, q_ref, k_ref, v_ref, do_ref, ke_ref, ve_ref, wk_ref, wv_ref, dq_ref, out_ref,
    key_true, raw_far, total_own, total_near, smooth, value, smooth_t, dk, dv, grad_out, grad_in,
    scaled, gathered, weights, acc,
    fwd_send, fwd_recv, w_send, w_recv, w_own, g_send, g_recv, s_send, s_recv,
):
    tokens = q_ref.shape[0]
    heads = k_ref.shape[1] // HEAD_SIZE
    D = HEAD_SIZE
    b = lax.axis_index("seq")
    h = lax.axis_index("head")
    rows = out_ref.shape[0]
    own = 2 * tokens

    def cols(g):
        return slice(g * D, (g + 1) * D)

    barrier = pltpu.get_barrier_semaphore()
    for d in (1, 2):
        for to in (lax.rem(b + d, n), lax.rem(b + n - d, n)):
            pl.semaphore_signal(barrier, inc=1, device_id={"seq": to}, device_id_type=MESH)
    for t in range(1, nh):
        pl.semaphore_signal(barrier, inc=1, device_id={"head": partner(h, t)}, device_id_type=MESH)
    pl.semaphore_wait(barrier, 4 + nh - 1)

    def along(src, dst, send, recv, step):
        return pltpu.make_async_remote_copy(
            src_ref=src, dst_ref=dst, send_sem=send, recv_sem=recv,
            device_id={"seq": lax.rem(b + n + step, n)}, device_id_type=MESH,
        )

    def across(src, dst, send, recv, t):
        return pltpu.make_async_remote_copy(
            src_ref=src, dst_ref=dst, send_sem=send, recv_sem=recv,
            device_id={"head": partner(h, t)}, device_id_type=MESH,
        )

    def when_start(condition, copies):
        @pl.when(condition)
        def _():
            for copy in copies:
                copy.start()

    weight_copies = []
    for t in list(range(2, nh)) + [1]:
        to = partner(h, t)
        for m, ref in enumerate((wk_ref, wv_ref)):
            copy = across(
                ref.at[pl.ds(to * rows, rows), :], weights.at[t, m],
                w_send.at[t, m], w_recv.at[t, m], t,
            )
            copy.start()
            weight_copies.append((t, copy))
    own_copies = []
    for m, ref in enumerate((wk_ref, wv_ref)):
        copy = pltpu.make_async_copy(ref.at[pl.ds(h * rows, rows), :], weights.at[0, m], w_own.at[m])
        copy.start()
        own_copies.append(copy)

    for j in range(tokens // SCALE_BLOCK):
        at = slice(j * SCALE_BLOCK, (j + 1) * SCALE_BLOCK)
        for g in range(heads):
            key_true[at, cols(g)] = (
                k_ref[at, cols(g)].astype(F32) * power_of_two(ke_ref[j, g])
            ).astype(BF16)
    key_far = along(key_true, raw_far, fwd_send.at[0], fwd_recv.at[0], 2)
    when_start(b + 2 < n, [key_far])
    keys_own = key_true[...]
    total_own[...] = jnp.broadcast_to(
        jnp.sum(keys_own.astype(F32), axis=0, keepdims=True), total_own.shape
    )
    sum_near = along(total_own, total_near, fwd_send.at[1], fwd_recv.at[1], 1)
    when_start(b + 1 < n, [sum_near])
    for j in range(tokens // SCALE_BLOCK):
        at = slice(j * SCALE_BLOCK, (j + 1) * SCALE_BLOCK)
        for g in range(heads):
            value[own + j * SCALE_BLOCK : own + (j + 1) * SCALE_BLOCK, cols(g)] = (
                v_ref[at, cols(g)].astype(F32) * power_of_two(ve_ref[j, g])
            ).astype(BF16)
    value_near = along(
        value.at[own : own + tokens], value.at[tokens:own], fwd_send.at[2], fwd_recv.at[2], 1
    )
    value_far = along(
        value.at[own : own + tokens], value.at[0:tokens], fwd_send.at[3], fwd_recv.at[3], 2
    )
    when_start(b + 1 < n, [value_near])
    when_start(b + 2 < n, [value_far])

    @pl.when(b < 1)
    def _():
        total_near[...] = jnp.zeros_like(total_near)
        value[tokens:own, :] = jnp.zeros((tokens, value.shape[1]), BF16)
        smooth[tokens:own, :] = jnp.zeros((tokens, value.shape[1]), BF16)

    @pl.when(b < 2)
    def _():
        raw_far[...] = jnp.zeros_like(raw_far)
        value[0:tokens, :] = jnp.zeros((tokens, value.shape[1]), BF16)
        smooth[0:tokens, :] = jnp.zeros((tokens, value.shape[1]), BF16)

    row_at = lax.broadcasted_iota(jnp.int32, (tokens, tokens), 0)
    col_at = lax.broadcasted_iota(jnp.int32, (tokens, tokens), 1)
    lower = jnp.where(row_at >= col_at, 1.0, 0.0).astype(BF16)
    running = jnp.dot(lower, keys_own, preferred_element_type=F32)
    place = b * tokens + lax.broadcasted_iota(jnp.int32, (tokens, 1), 0)
    counts = jnp.clip(place + 1, 1, ATTEND_WINDOW).astype(F32)

    @pl.when(b >= 1)
    def _():
        sum_near.wait_recv()

    @pl.when(b >= 2)
    def _():
        key_far.wait_recv()

    far = jnp.dot(lower, raw_far[...], preferred_element_type=F32)
    mean = (running - far + far[tokens - 1 :, :] + total_near[0:1, :]) / counts
    smooth[own : own + tokens, :] = (keys_own.astype(F32) - mean).astype(BF16)
    smooth_near = along(
        smooth.at[own : own + tokens], smooth.at[tokens:own], fwd_send.at[4], fwd_recv.at[4], 1
    )
    smooth_far = along(
        smooth.at[own : own + tokens], smooth.at[0:tokens], fwd_send.at[5], fwd_recv.at[5], 2
    )
    when_start(b + 1 < n, [smooth_near])
    when_start(b + 2 < n, [smooth_far])
    dk[...] = jnp.zeros_like(dk)
    dv[...] = jnp.zeros_like(dv)

    @pl.when(b >= 1)
    def _():
        value_near.wait_recv()
        smooth_near.wait_recv()

    @pl.when(b >= 2)
    def _():
        value_far.wait_recv()
        smooth_far.wait_recv()

    tile = SCALE_BLOCK
    span = ATTEND_WINDOW + tile
    scale = QUERY_SCALE ** (-0.5)
    group = q_ref.shape[1] // (heads * D)
    width = group * tile
    key_row = lax.broadcasted_iota(jnp.int32, (ATTEND_WINDOW, width), 0)
    near_row = lax.broadcasted_iota(jnp.int32, (tile, width), 0)
    lane = lax.rem(lax.broadcasted_iota(jnp.int32, (1, width), 1), tile)

    grad_copies = []
    for g in range(heads):
        smooth_t[...] = smooth[:, cols(g)].astype(F32).T.astype(BF16)

        def one_tile(i, carry, g=g):
            begin = pl.multiple_of(i * tile, tile)
            at = pl.ds(begin, tile)
            window = pl.ds(begin, span)
            q = jnp.concatenate([q_ref[at, cols(g * group + u)] for u in range(group)], 0)
            do = jnp.concatenate([do_ref[at, cols(g * group + u)] for u in range(group)], 0)
            keys = smooth[window, cols(g)]
            values = value[window, cols(g)]
            scores = contract_last(keys, q)
            first = jnp.maximum(lane + 1, (2 - b) * tokens - begin)
            scores = jnp.concatenate(
                [
                    jnp.where(key_row >= first, scores[:ATTEND_WINDOW], -jnp.inf),
                    jnp.where(near_row <= lane, scores[ATTEND_WINDOW:], -jnp.inf),
                ],
                0,
            )
            highest = jnp.max(scores, axis=0, keepdims=True)
            powers = jnp.exp2((scores - highest) * (scale * LOG2_E))
            shares = powers * (1.0 / jnp.sum(powers, axis=0, keepdims=True))
            rounded = shares.astype(BF16)
            share_grad = contract_last(values, do)
            row_dot = jnp.sum(rounded.astype(F32) * share_grad, axis=0, keepdims=True)
            score_grad = (shares * (share_grad - row_dot)).astype(BF16)
            dv[g, window, :] += jnp.dot(rounded, do, preferred_element_type=F32)
            dk[g, window, :] += jnp.dot(score_grad, q, preferred_element_type=F32)
            dq = jnp.dot(smooth_t[:, window], score_grad, preferred_element_type=F32) * scale
            dq = dq.T.astype(BF16)
            for u in range(group):
                dq_ref[at, cols(g * group + u)] = dq[u * tile : (u + 1) * tile]
            return carry

        lax.fori_loop(0, tokens // tile, one_tile, 0)
        for d in (2, 1):
            part = slice((2 - d) * tokens, (3 - d) * tokens)
            grad_out[g, d - 1, :, :D] = (dk[g, part, :] * scale).astype(BF16)
            grad_out[g, d - 1, :, D:] = dv[g, part, :].astype(BF16)
            copy = along(
                grad_out.at[g, d - 1], grad_in.at[g, d - 1],
                g_send.at[g, d - 1], g_recv.at[g, d - 1], -d,
            )
            when_start(b >= d, [copy])
            grad_copies.append((d, copy))

    share_copies = []
    for g in range(heads):
        for d in (1, 2):
            copy = grad_copies[g * 2 + (2 - d)][1]

            @pl.when(b + d < n)
            def _(copy=copy):
                copy.wait_recv()

            @pl.when(b + d >= n)
            def _(g=g, d=d):
                grad_in[g, d - 1] = jnp.zeros(grad_in.shape[2:], BF16)

        for j in range(tokens // SCALE_BLOCK):
            at = slice(j * SCALE_BLOCK, (j + 1) * SCALE_BLOCK)
            here = slice(own + j * SCALE_BLOCK, own + (j + 1) * SCALE_BLOCK)
            for m, (ref, exponent, factor) in enumerate(
                ((dk, ke_ref, scale), (dv, ve_ref, 1.0))
            ):
                whole = ref[g, here, :] * factor
                for d in (1, 2):
                    whole = whole + grad_in[g, d - 1, at, cols(m)].astype(F32)
                scaled[g, at, cols(m)] = (whole * power_of_two(exponent[j, g])).astype(BF16)
        for t in list(range(2, nh)) + [1]:
            copy = across(
                scaled.at[g], gathered.at[t - 1, g], s_send.at[t - 1, g], s_recv.at[t - 1, g], t
            )
            copy.start()
            share_copies.append((t, copy))

    chunk = rows // 4

    def product(t, at):
        total = None
        for g in range(heads):
            left = jnp.concatenate([weights[t, 0, at, cols(g)], weights[t, 1, at, cols(g)]], 1)
            right = scaled[g] if t == 0 else gathered[t - 1, g]
            term = contract_last(left, right)
            total = term if total is None else total + term
        return total

    for copy in own_copies:
        copy.wait()
    for t in range(nh):
        for source, copy in weight_copies + share_copies:
            if source == t:
                copy.wait_recv()

        def one_chunk(c, carry, t=t):
            at = pl.ds(pl.multiple_of(c * chunk, 16), chunk)
            total = product(t, at)
            if t > 0:
                total = total + acc[at, :]
            if t < nh - 1:
                acc[at, :] = total
            else:
                out_ref[at, :] = total.astype(BF16)
            return carry

        lax.fori_loop(0, 4, one_chunk, 0)

    @pl.when(b + 1 < n)
    def _():
        for copy in (sum_near, value_near, smooth_near):
            copy.wait_send()

    @pl.when(b + 2 < n)
    def _():
        for copy in (key_far, value_far, smooth_far):
            copy.wait_send()

    for d, copy in grad_copies:
        @pl.when(b >= d)
        def _(copy=copy):
            copy.wait_send()

    for _, copy in weight_copies + share_copies:
        copy.wait_send()


def solution(mesh):
    n, nh = mesh.shape["seq"], mesh.shape["head"]

    def local(q, k, v, do, ke, ve, wk, wv):
        tokens, width = k.shape
        heads = width // HEAD_SIZE
        assert ATTEND_WINDOW == 2 * tokens
        rows = wk.shape[0] // nh
        vmem = pl.BlockSpec(memory_space=pltpu.VMEM)
        smem = pl.BlockSpec(memory_space=pltpu.SMEM)
        hbm = pl.BlockSpec(memory_space=pl.ANY)
        dma = pltpu.SemaphoreType.DMA
        return pl.pallas_call(
            functools.partial(kernel, n, nh),
            out_shape=(
                jax.ShapeDtypeStruct(q.shape, BF16),
                jax.ShapeDtypeStruct((rows, tokens), BF16),
            ),
            in_specs=[vmem, vmem, vmem, vmem, smem, smem, hbm, hbm],
            out_specs=(vmem, vmem),
            scratch_shapes=[
                pltpu.VMEM((tokens, width), BF16),
                pltpu.VMEM((tokens, width), BF16),
                pltpu.VMEM((8, width), F32),
                pltpu.VMEM((8, width), F32),
                pltpu.VMEM((3 * tokens, width), BF16),
                pltpu.VMEM((3 * tokens, width), BF16),
                pltpu.VMEM((HEAD_SIZE, 3 * tokens), BF16),
                pltpu.VMEM((heads, 3 * tokens, HEAD_SIZE), F32),
                pltpu.VMEM((heads, 3 * tokens, HEAD_SIZE), F32),
                pltpu.VMEM((heads, 2, tokens, 2 * HEAD_SIZE), BF16),
                pltpu.VMEM((heads, 2, tokens, 2 * HEAD_SIZE), BF16),
                pltpu.VMEM((heads, tokens, 2 * HEAD_SIZE), BF16),
                pltpu.VMEM((nh - 1, heads, tokens, 2 * HEAD_SIZE), BF16),
                pltpu.VMEM((nh, 2, rows, width), BF16),
                pltpu.VMEM((rows, tokens), F32),
                dma((6,)), dma((6,)),
                dma((nh, 2)), dma((nh, 2)), dma((2,)),
                dma((heads, 2)), dma((heads, 2)),
                dma((nh - 1, heads)), dma((nh - 1, heads)),
            ],
            compiler_params=pltpu.CompilerParams(
                collective_id=0, has_side_effects=True, vmem_limit_bytes=56 * 2**20
            ),
        )(q, k, v, do, ke, ve, wk, wv)

    in_specs = (P("seq", "head"),) * 6 + (P(None, "head"),) * 2
    out_specs = (P("seq", "head"), P("head", "seq"))
    return jax.shard_map(local, mesh=mesh, in_specs=in_specs, out_specs=out_specs, check_vma=False)
```

time: 196 us -> 102 us (0.52)
  Pallas kernels: 0 us -> 93.1 us
  waiting for transfers between devices: 73 us -> 0 us
  starting transfers between devices: 33.1 us -> 0 us
  matrix products: 31.3 us -> 0 us
  other arithmetic: 18.5 us -> 0 us
  local copies, waits for them, and re-layouts: 24.4 us -> 7.04 us
  between operations: 14.3 us -> 0.64 us
    pallas_call x0 -> x1, Pallas kernels: none -> 93.1 us  [local(): pl.pallas_call(functools.partial(kernel, n, nh), out_shape=(jax.ShapeDtyp...]
    unnamed x2 -> x0, waiting for transfers between devices: 54.6 us -> none
    ppermute x10 -> x0, starting transfers between devices: 33 us -> none  [passed_along(): lax.ppermute(value, axis, [(source, source + steps) for source in range(f...]
    dot_general x13 -> x0, matrix products: 18.9 us -> none  [the longest x1 4.1 us: local(): jnp.dot(key_matrix, key_columns, preferred_element_type=jnp.float32)]
    ppermute x10 -> x0, waiting for transfers between devices: 18.4 us -> none  [passed_along(): lax.ppermute(value, axis, [(source, source + steps) for source in range(f...]
    sub x2 -> x0, matrix products: 12.4 us -> none  [one_head(): weights = jnp.exp(scores - highest)]
    convert_element_type x6 -> x0, other arithmetic: 9.4 us -> none  [the longest x2 7.51 us: one_head(): rounded = shares.astype(jnp.bfloat16)]
    unnamed x25 -> x4, local copies, waits for them, and re-layouts: 13.6 us -> 7.04 us
  transfers between devices with their start and end apart: 11 -> 0, of which waited for: 5 -> 0; matrix products, arithmetic and copies ran while one was open for 7% -> 0% of each run, Pallas kernels for 0% -> 0%
where the time goes in v1:
time: 102 us; the launch traced here: 101 us
  Pallas kernels  93.1 us (91%)
  local copies, waits for them, and re-layouts  7.04 us (7%)
    pallas_call x1, Pallas kernels, local(): pl.pallas_call(functools.partial(kernel, n, nh), out_shape=(jax.ShapeDtyp...  93.1 us
    unnamed x4, local copies, waits for them, and re-layouts  7.04 us

profile of v1, /device:TPU:0, one launch (start us, length us, event | category | flops | bytes accessed | tf_op | source)
XLA Modules:
  0.0 100.8 jit_solution(16444284086604726278)
XLA Ops:
  0.6 1.3 %copy.10.ke_ref = s32[4,2]{1,0:T(4,128)} copy(s32[4,2]{0,1:T(2,128)} %param.12) | data formatting | bytes 64 | tf_op args[4]
  2.0 1.3 %copy.11.ve_ref = s32[4,2]{1,0:T(4,128)} copy(s32[4,2]{0,1:T(2,128)} %param.13) | data formatting | bytes 64 | tf_op args[5]
  3.3 93.1 %shard_map.95 = (bf16[512,512]{1,0:T(8,128)(2,1)}, bf16[1344,512]{1,0:T(8,128)(2,1)}) custom-call(bf16[512,512]{1,0:T(8,128)(2,1)} %q_ref.1, bf16[512,256]{1,0:T(8,128)(2,1)} %k_ref.1, bf16[512,256]{1,0:T(8,128)(2,1)} %v_ref.1, bf16[512,512]{1,0:T(8,128)(2,1)} %do_ref.1, s32[4,2]{1,0:T(4,128)} %copy.10.ke_ref, s32[4,2]{1,0:T(4,128)} %copy.11.ve_ref, ...), custom_call_target="tpu_custom_call" | custom-call | tf_op jit(solution)/shard_map/pallas_call | solution.py:325
  96.4 1.9 %copy.14 = bf16[512,512]{1,0:T(8,128)(2,1)} copy(bf16[512,512]{1,0:T(8,128)(2,1)} %get-tuple-element.4) | data formatting | bytes 1048576
  98.3 2.5 %copy.15 = bf16[1344,512]{1,0:T(8,128)(2,1)} copy(bf16[1344,512]{1,0:T(8,128)(2,1)} %get-tuple-element.5) | data formatting | bytes 2752512

commit v2 on v1

--- a/solution.py
+++ b/solution.py
@@ -38,7 +38,7 @@
     n, nh, q_ref, k_ref, v_ref, do_ref, ke_ref, ve_ref, wk_ref, wv_ref, dq_ref, out_ref,
     key_true, raw_far, total_own, total_near, smooth, value, smooth_t, dk, dv, grad_out, grad_in,
     scaled, gathered, weights, acc,
-    fwd_send, fwd_recv, w_send, w_recv, w_own, g_send, g_recv, s_send, s_recv,
+    fwd_send, fwd_recv, w_send, w_recv, y_send, y_recv, w_own, g_send, g_recv, far_send, far_recv, s_send, s_recv,
 ):
     tokens = q_ref.shape[0]
     heads = k_ref.shape[1] // HEAD_SIZE
@@ -77,16 +77,32 @@
             for copy in copies:
                 copy.start()
 
-    weight_copies = []
+    half = rows // 2
+    mine = lax.rem(b, 2) * half
+    weight_copies, pair_copies = [], []
     for t in list(range(2, nh)) + [1]:
         to = partner(h, t)
         for m, ref in enumerate((wk_ref, wv_ref)):
-            copy = across(
-                ref.at[pl.ds(to * rows, rows), :], weights.at[t, m],
-                w_send.at[t, m], w_recv.at[t, m], t,
-            )
+            if t == 1:
+                src, dst = ref.at[pl.ds(to * rows, rows), :], weights.at[t, m]
+            else:
+                src = ref.at[pl.ds(to * rows + mine, half), :]
+                dst = weights.at[t, m, pl.ds(mine, half), :]
+                pair_copies.append(
+                    pltpu.make_async_remote_copy(
+                        src_ref=dst, dst_ref=dst, send_sem=y_send.at[t, m], recv_sem=y_recv.at[t, m],
+                        device_id={"seq": partner(b, 1)}, device_id_type=MESH,
+                    )
+                )
+            copy = across(src, dst, w_send.at[t, m], w_recv.at[t, m], t)
             copy.start()
             weight_copies.append((t, copy))
+
+    def hand_over(first, last):
+        for at in range(first, min(last, len(pair_copies))):
+            weight_copies[at][1].wait_recv()
+            pair_copies[at].start()
+
     own_copies = []
     for m, ref in enumerate((wk_ref, wv_ref)):
         copy = pltpu.make_async_copy(ref.at[pl.ds(h * rows, rows), :], weights.at[0, m], w_own.at[m])
@@ -110,29 +126,39 @@
     for j in range(tokens // SCALE_BLOCK):
         at = slice(j * SCALE_BLOCK, (j + 1) * SCALE_BLOCK)
         for g in range(heads):
-            value[own + j * SCALE_BLOCK : own + (j + 1) * SCALE_BLOCK, cols(g)] = (
+            value[g, own + j * SCALE_BLOCK : own + (j + 1) * SCALE_BLOCK, :] = (
                 v_ref[at, cols(g)].astype(F32) * power_of_two(ve_ref[j, g])
             ).astype(BF16)
-    value_near = along(
-        value.at[own : own + tokens], value.at[tokens:own], fwd_send.at[2], fwd_recv.at[2], 1
-    )
-    value_far = along(
-        value.at[own : own + tokens], value.at[0:tokens], fwd_send.at[3], fwd_recv.at[3], 2
-    )
-    when_start(b + 1 < n, [value_near])
-    when_start(b + 2 < n, [value_far])
+
+    def halo(ref, g, kind):
+        src = ref.at[g, own : own + tokens]
+        at = 2 + 4 * g + 2 * kind
+        return (
+            along(src, ref.at[g, tokens:own], fwd_send.at[at], fwd_recv.at[at], 1),
+            along(src, ref.at[g, 0:tokens], fwd_send.at[at + 1], fwd_recv.at[at + 1], 2),
+        )
+
+    halos = [(halo(value, g, 0), halo(smooth, g, 1)) for g in range(heads)]
+
+    def send_halo(copies):
+        when_start(b + 2 < n, [copies[1]])
+        when_start(b + 1 < n, [copies[0]])
+
+    send_halo(halos[0][0])
 
     @pl.when(b < 1)
     def _():
         total_near[...] = jnp.zeros_like(total_near)
-        value[tokens:own, :] = jnp.zeros((tokens, value.shape[1]), BF16)
-        smooth[tokens:own, :] = jnp.zeros((tokens, value.shape[1]), BF16)
+        for g in range(heads):
+            value[g, tokens:own, :] = jnp.zeros((tokens, D), BF16)
+            smooth[g, tokens:own, :] = jnp.zeros((tokens, D), BF16)
 
     @pl.when(b < 2)
     def _():
         raw_far[...] = jnp.zeros_like(raw_far)
-        value[0:tokens, :] = jnp.zeros((tokens, value.shape[1]), BF16)
-        smooth[0:tokens, :] = jnp.zeros((tokens, value.shape[1]), BF16)
+        for g in range(heads):
+            value[g, 0:tokens, :] = jnp.zeros((tokens, D), BF16)
+            smooth[g, 0:tokens, :] = jnp.zeros((tokens, D), BF16)
 
     row_at = lax.broadcasted_iota(jnp.int32, (tokens, tokens), 0)
     col_at = lax.broadcasted_iota(jnp.int32, (tokens, tokens), 1)
@@ -151,27 +177,15 @@
 
     far = jnp.dot(lower, raw_far[...], preferred_element_type=F32)
     mean = (running - far + far[tokens - 1 :, :] + total_near[0:1, :]) / counts
-    smooth[own : own + tokens, :] = (keys_own.astype(F32) - mean).astype(BF16)
-    smooth_near = along(
-        smooth.at[own : own + tokens], smooth.at[tokens:own], fwd_send.at[4], fwd_recv.at[4], 1
-    )
-    smooth_far = along(
-        smooth.at[own : own + tokens], smooth.at[0:tokens], fwd_send.at[5], fwd_recv.at[5], 2
-    )
-    when_start(b + 1 < n, [smooth_near])
-    when_start(b + 2 < n, [smooth_far])
+    smoothed = (keys_own.astype(F32) - mean).astype(BF16)
+    for g in range(heads):
+        smooth[g, own : own + tokens, :] = smoothed[:, cols(g)]
+    send_halo(halos[0][1])
+    for g in range(1, heads):
+        send_halo(halos[g][0])
+        send_halo(halos[g][1])
     dk[...] = jnp.zeros_like(dk)
     dv[...] = jnp.zeros_like(dv)
-
-    @pl.when(b >= 1)
-    def _():
-        value_near.wait_recv()
-        smooth_near.wait_recv()
-
-    @pl.when(b >= 2)
-    def _():
-        value_far.wait_recv()
-        smooth_far.wait_recv()
 
     tile = SCALE_BLOCK
     span = ATTEND_WINDOW + tile
@@ -182,9 +196,29 @@
     near_row = lax.broadcasted_iota(jnp.int32, (tile, width), 0)
     lane = lax.rem(lax.broadcasted_iota(jnp.int32, (1, width), 1), tile)
 
-    grad_copies = []
+    def far_grad(g, i):
+        at = pl.ds(pl.multiple_of(i * tile, tile), tile)
+        return along(
+            grad_out.at[g, 1, at, :], grad_in.at[g, 1, at, :], far_send.at[g, i], far_recv.at[g, i], -2
+        )
+
+    def put_grad(g, d, at, window):
+        grad_out[g, d - 1, at, :D] = (dk[g, window, :] * scale).astype(BF16)
+        grad_out[g, d - 1, at, D:] = dv[g, window, :].astype(BF16)
+
+    near_copies = []
     for g in range(heads):
-        smooth_t[...] = smooth[:, cols(g)].astype(F32).T.astype(BF16)
+        @pl.when(b >= 1)
+        def _(g=g):
+            for copies in halos[g]:
+                copies[0].wait_recv()
+
+        @pl.when(b >= 2)
+        def _(g=g):
+            for copies in halos[g]:
+                copies[1].wait_recv()
+
+        smooth_t[...] = smooth[g].astype(F32).T.astype(BF16)
 
         def one_tile(i, carry, g=g):
             begin = pl.multiple_of(i * tile, tile)
@@ -192,8 +226,8 @@
             window = pl.ds(begin, span)
             q = jnp.concatenate([q_ref[at, cols(g * group + u)] for u in range(group)], 0)
             do = jnp.concatenate([do_ref[at, cols(g * group + u)] for u in range(group)], 0)
-            keys = smooth[window, cols(g)]
-            values = value[window, cols(g)]
+            keys = smooth[g, window, :]
+            values = value[g, window, :]
             scores = contract_last(keys, q)
             first = jnp.maximum(lane + 1, (2 - b) * tokens - begin)
             scores = jnp.concatenate(
@@ -216,32 +250,37 @@
             dq = dq.T.astype(BF16)
             for u in range(group):
                 dq_ref[at, cols(g * group + u)] = dq[u * tile : (u + 1) * tile]
+            put_grad(g, 2, at, at)
+            when_start(b >= 2, [far_grad(g, i)])
             return carry
 
         lax.fori_loop(0, tokens // tile, one_tile, 0)
-        for d in (2, 1):
-            part = slice((2 - d) * tokens, (3 - d) * tokens)
-            grad_out[g, d - 1, :, :D] = (dk[g, part, :] * scale).astype(BF16)
-            grad_out[g, d - 1, :, D:] = dv[g, part, :].astype(BF16)
-            copy = along(
-                grad_out.at[g, d - 1], grad_in.at[g, d - 1],
-                g_send.at[g, d - 1], g_recv.at[g, d - 1], -d,
-            )
-            when_start(b >= d, [copy])
-            grad_copies.append((d, copy))
+        put_grad(g, 1, slice(0, tokens), slice(tokens, own))
+        copy = along(grad_out.at[g, 0], grad_in.at[g, 0], g_send.at[g], g_recv.at[g], -1)
+        when_start(b >= 1, [copy])
+        near_copies.append(copy)
+        share = -(-len(pair_copies) // heads)
+        hand_over(g * share, (g + 1) * share)
 
     share_copies = []
+    onward = []
     for g in range(heads):
-        for d in (1, 2):
-            copy = grad_copies[g * 2 + (2 - d)][1]
-
-            @pl.when(b + d < n)
-            def _(copy=copy):
-                copy.wait_recv()
-
-            @pl.when(b + d >= n)
-            def _(g=g, d=d):
-                grad_in[g, d - 1] = jnp.zeros(grad_in.shape[2:], BF16)
+        @pl.when(b + 1 < n)
+        def _(g=g):
+            near_copies[g].wait_recv()
+
+        @pl.when(b + 1 >= n)
+        def _(g=g):
+            grad_in[g, 0] = jnp.zeros(grad_in.shape[2:], BF16)
+
+        @pl.when(b + 2 < n)
+        def _(g=g):
+            for i in range(tokens // tile):
+                far_grad(g, i).wait_recv()
+
+        @pl.when(b + 2 >= n)
+        def _(g=g):
+            grad_in[g, 1] = jnp.zeros(grad_in.shape[2:], BF16)
 
         for j in range(tokens // SCALE_BLOCK):
             at = slice(j * SCALE_BLOCK, (j + 1) * SCALE_BLOCK)
@@ -253,12 +292,23 @@
                 for d in (1, 2):
                     whole = whole + grad_in[g, d - 1, at, cols(m)].astype(F32)
                 scaled[g, at, cols(m)] = (whole * power_of_two(exponent[j, g])).astype(BF16)
-        for t in list(range(2, nh)) + [1]:
+        for t in list(range(2, nh, 2)) + [1]:
             copy = across(
                 scaled.at[g], gathered.at[t - 1, g], s_send.at[t - 1, g], s_recv.at[t - 1, g], t
             )
             copy.start()
             share_copies.append((t, copy))
+            if t > 1:
+                onward.append(
+                    (
+                        t,
+                        copy,
+                        across(
+                            gathered.at[t - 1, g], gathered.at[t, g],
+                            s_send.at[t, g], s_recv.at[t, g], 1,
+                        ),
+                    )
+                )
 
     chunk = rows // 4
 
@@ -274,8 +324,21 @@
     for copy in own_copies:
         copy.wait()
     for t in range(nh):
-        for source, copy in weight_copies + share_copies:
+        if t == 2:
+            for copy in pair_copies:
+                copy.wait_recv()
+        if t == 1:
+            for source, copy in weight_copies:
+                if source == 1:
+                    copy.wait_recv()
+            for source, copy in share_copies:
+                if source == 1:
+                    copy.wait_recv()
+        for source, arrived, copy in onward:
             if source == t:
+                arrived.wait_recv()
+                copy.start()
+            if source == t - 1:
                 copy.wait_recv()
 
         def one_chunk(c, carry, t=t):
@@ -293,20 +356,34 @@
 
     @pl.when(b + 1 < n)
     def _():
-        for copy in (sum_near, value_near, smooth_near):
+        sum_near.wait_send()
+        for pair in halos:
+            for copies in pair:
+                copies[0].wait_send()
+
+    @pl.when(b + 2 < n)
+    def _():
+        key_far.wait_send()
+        for pair in halos:
+            for copies in pair:
+                copies[1].wait_send()
+
+    @pl.when(b >= 1)
+    def _():
+        for copy in near_copies:
             copy.wait_send()
 
-    @pl.when(b + 2 < n)
-    def _():
-        for copy in (key_far, value_far, smooth_far):
-            copy.wait_send()
-
-    for d, copy in grad_copies:
-        @pl.when(b >= d)
-        def _(copy=copy):
-            copy.wait_send()
+    @pl.when(b >= 2)
+    def _():
+        for g in range(heads):
+            for i in range(tokens // tile):
+                far_grad(g, i).wait_send()
 
     for _, copy in weight_copies + share_copies:
+        copy.wait_send()
+    for copy in pair_copies:
+        copy.wait_send()
+    for _, _, copy in onward:
         copy.wait_send()
 
 
@@ -335,8 +412,8 @@
                 pltpu.VMEM((tokens, width), BF16),
                 pltpu.VMEM((8, width), F32),
                 pltpu.VMEM((8, width), F32),
-                pltpu.VMEM((3 * tokens, width), BF16),
-                pltpu.VMEM((3 * tokens, width), BF16),
+                pltpu.VMEM((heads, 3 * tokens, HEAD_SIZE), BF16),
+                pltpu.VMEM((heads, 3 * tokens, HEAD_SIZE), BF16),
                 pltpu.VMEM((HEAD_SIZE, 3 * tokens), BF16),
                 pltpu.VMEM((heads, 3 * tokens, HEAD_SIZE), F32),
                 pltpu.VMEM((heads, 3 * tokens, HEAD_SIZE), F32),
@@ -346,9 +423,10 @@
                 pltpu.VMEM((nh - 1, heads, tokens, 2 * HEAD_SIZE), BF16),
                 pltpu.VMEM((nh, 2, rows, width), BF16),
                 pltpu.VMEM((rows, tokens), F32),
-                dma((6,)), dma((6,)),
-                dma((nh, 2)), dma((nh, 2)), dma((2,)),
-                dma((heads, 2)), dma((heads, 2)),
+                dma((2 + 4 * heads,)), dma((2 + 4 * heads,)),
+                dma((nh, 2)), dma((nh, 2)), dma((nh, 2)), dma((nh, 2)), dma((2,)),
+                dma((heads,)), dma((heads,)),
+                dma((heads, tokens // SCALE_BLOCK)), dma((heads, tokens // SCALE_BLOCK)),
                 dma((nh - 1, heads)), dma((nh - 1, heads)),
             ],
             compiler_params=pltpu.CompilerParams(

time: 102 us -> 86.6 us (0.85)
  the two profiles are of different devices: /device:TPU:0 before, /device:TPU:9 now
where the time goes in v2:
time: 86.6 us; the launch traced here: 86.3 us
  Pallas kernels  78.7 us (91%)
  local copies, waits for them, and re-layouts  7.04 us (8%)
    pallas_call x1, Pallas kernels, local(): pl.pallas_call(functools.partial(kernel, n, nh), out_shape=(jax.ShapeDtyp...  78.7 us
    unnamed x4, local copies, waits for them, and re-layouts  7.04 us

profile of v2, /device:TPU:9, one launch (start us, length us, event | category | flops | bytes accessed | tf_op | source)
XLA Modules:
  0.0 86.3 jit_solution(9343012334450389365)
XLA Ops:
  0.6 1.3 %copy.10.ke_ref = s32[4,2]{1,0:T(4,128)} copy(s32[4,2]{0,1:T(2,128)} %param.12) | data formatting | bytes 64 | tf_op args[4]
  2.0 1.3 %copy.11.ve_ref = s32[4,2]{1,0:T(4,128)} copy(s32[4,2]{0,1:T(2,128)} %param.13) | data formatting | bytes 64 | tf_op args[5]
  3.3 78.7 %shard_map.95 = (bf16[512,512]{1,0:T(8,128)(2,1)}, bf16[1344,512]{1,0:T(8,128)(2,1)}) custom-call(bf16[512,512]{1,0:T(8,128)(2,1)} %q_ref.1, bf16[512,256]{1,0:T(8,128)(2,1)} %k_ref.1, bf16[512,256]{1,0:T(8,128)(2,1)} %v_ref.1, bf16[512,512]{1,0:T(8,128)(2,1)} %do_ref.1, s32[4,2]{1,0:T(4,128)} %copy.10.ke_ref, s32[4,2]{1,0:T(4,128)} %copy.11.ve_ref, ...), custom_call_target="tpu_custom_call" | custom-call | tf_op jit(solution)/shard_map/pallas_call | solution.py:402
  82.0 1.9 %copy.14 = bf16[512,512]{1,0:T(8,128)(2,1)} copy(bf16[512,512]{1,0:T(8,128)(2,1)} %get-tuple-element.4) | data formatting | bytes 1048576
  83.8 2.5 %copy.15 = bf16[1344,512]{1,0:T(8,128)(2,1)} copy(bf16[1344,512]{1,0:T(8,128)(2,1)} %get-tuple-element.5) | data formatting | bytes 2752512

commit v3 on v2

--- a/solution.py
+++ b/solution.py
@@ -113,7 +113,7 @@
         at = slice(j * SCALE_BLOCK, (j + 1) * SCALE_BLOCK)
         for g in range(heads):
             key_true[at, cols(g)] = (
-                k_ref[at, cols(g)].astype(F32) * power_of_two(ke_ref[j, g])
+                k_ref[at, cols(g)].astype(F32) * power_of_two(ke_ref[j : j + 1, g : g + 1])
             ).astype(BF16)
     key_far = along(key_true, raw_far, fwd_send.at[0], fwd_recv.at[0], 2)
     when_start(b + 2 < n, [key_far])
@@ -127,7 +127,7 @@
         at = slice(j * SCALE_BLOCK, (j + 1) * SCALE_BLOCK)
         for g in range(heads):
             value[g, own + j * SCALE_BLOCK : own + (j + 1) * SCALE_BLOCK, :] = (
-                v_ref[at, cols(g)].astype(F32) * power_of_two(ve_ref[j, g])
+                v_ref[at, cols(g)].astype(F32) * power_of_two(ve_ref[j : j + 1, g : g + 1])
             ).astype(BF16)
 
     def halo(ref, g, kind):
@@ -136,14 +136,17 @@
         return (
             along(src, ref.at[g, tokens:own], fwd_send.at[at], fwd_recv.at[at], 1),
             along(src, ref.at[g, 0:tokens], fwd_send.at[at + 1], fwd_recv.at[at + 1], 2),
+            along(ref.at[g, 0:tokens], ref.at[g, tokens:own], fwd_send.at[at], fwd_recv.at[at], -1),
         )
 
     halos = [(halo(value, g, 0), halo(smooth, g, 1)) for g in range(heads)]
 
     def send_halo(copies):
         when_start(b + 2 < n, [copies[1]])
-        when_start(b + 1 < n, [copies[0]])
-
+        when_start(even, [copies[0]])
+
+    even = lax.rem(b, 2) == 0
+    passes_on = jnp.logical_and(lax.rem(b, 2) == 1, b >= 2)
     send_halo(halos[0][0])
 
     @pl.when(b < 1)
@@ -208,15 +211,17 @@
 
     near_copies = []
     for g in range(heads):
+        for copies in halos[g]:
+            @pl.when(b >= 2)
+            def _(copies=copies):
+                copies[1].wait_recv()
+
+            when_start(passes_on, [copies[2]])
+
         @pl.when(b >= 1)
         def _(g=g):
             for copies in halos[g]:
                 copies[0].wait_recv()
-
-        @pl.when(b >= 2)
-        def _(g=g):
-            for copies in halos[g]:
-                copies[1].wait_recv()
 
         smooth_t[...] = smooth[g].astype(F32).T.astype(BF16)
 
@@ -291,7 +296,7 @@
                 whole = ref[g, here, :] * factor
                 for d in (1, 2):
                     whole = whole + grad_in[g, d - 1, at, cols(m)].astype(F32)
-                scaled[g, at, cols(m)] = (whole * power_of_two(exponent[j, g])).astype(BF16)
+                scaled[g, at, cols(m)] = (whole * power_of_two(exponent[j : j + 1, g : g + 1])).astype(BF16)
         for t in list(range(2, nh, 2)) + [1]:
             copy = across(
                 scaled.at[g], gathered.at[t - 1, g], s_send.at[t - 1, g], s_recv.at[t - 1, g], t
@@ -357,9 +362,18 @@
     @pl.when(b + 1 < n)
     def _():
         sum_near.wait_send()
+
+    @pl.when(even)
+    def _():
         for pair in halos:
             for copies in pair:
                 copies[0].wait_send()
+
+    @pl.when(passes_on)
+    def _():
+        for pair in halos:
+            for copies in pair:
+                copies[2].wait_send()
 
     @pl.when(b + 2 < n)
     def _():
@@ -393,10 +407,9 @@
     def local(q, k, v, do, ke, ve, wk, wv):
         tokens, width = k.shape
         heads = width // HEAD_SIZE
-        assert ATTEND_WINDOW == 2 * tokens
+        assert ATTEND_WINDOW == 2 * tokens and n % 2 == 0
         rows = wk.shape[0] // nh
         vmem = pl.BlockSpec(memory_space=pltpu.VMEM)
-        smem = pl.BlockSpec(memory_space=pltpu.SMEM)
         hbm = pl.BlockSpec(memory_space=pl.ANY)
         dma = pltpu.SemaphoreType.DMA
         return pl.pallas_call(
@@ -405,7 +418,7 @@
                 jax.ShapeDtypeStruct(q.shape, BF16),
                 jax.ShapeDtypeStruct((rows, tokens), BF16),
             ),
-            in_specs=[vmem, vmem, vmem, vmem, smem, smem, hbm, hbm],
+            in_specs=[vmem, vmem, vmem, vmem, vmem, vmem, hbm, hbm],
             out_specs=(vmem, vmem),
             scratch_shapes=[
                 pltpu.VMEM((tokens, width), BF16),

time: 86.6 us -> 88.1 us (1.017)
  the two profiles are of different devices: /device:TPU:9 before, /device:TPU:13 now
where the time goes in v3:
time: 88.1 us; the launch traced here: 87.8 us
  Pallas kernels  80.1 us (91%)
  local copies, waits for them, and re-layouts  7.04 us (8%)
    pallas_call x1, Pallas kernels, local(): pl.pallas_call(functools.partial(kernel, n, nh), out_shape=(jax.ShapeDtyp...  80.1 us
    unnamed x4, local copies, waits for them, and re-layouts  7.04 us

profile of v3, /device:TPU:13, one launch (start us, length us, event | category | flops | bytes accessed | tf_op | source)
XLA Modules:
  0.0 87.8 jit_solution(9895589627615551469)
XLA Ops:
  0.6 1.3 %copy.10.ke_ref = s32[4,2]{1,0:T(4,128)} copy(s32[4,2]{0,1:T(2,128)} %param.12) | data formatting | bytes 64 | tf_op args[4]
  2.0 1.3 %copy.11.ve_ref = s32[4,2]{1,0:T(4,128)} copy(s32[4,2]{0,1:T(2,128)} %param.13) | data formatting | bytes 64 | tf_op args[5]
  3.3 80.1 %shard_map.95 = (bf16[512,512]{1,0:T(8,128)(2,1)}, bf16[1344,512]{1,0:T(8,128)(2,1)}) custom-call(bf16[512,512]{1,0:T(8,128)(2,1)} %q_ref.1, bf16[512,256]{1,0:T(8,128)(2,1)} %k_ref.1, bf16[512,256]{1,0:T(8,128)(2,1)} %v_ref.1, bf16[512,512]{1,0:T(8,128)(2,1)} %do_ref.1, s32[4,2]{1,0:T(4,128)} %copy.10.ke_ref, s32[4,2]{1,0:T(4,128)} %copy.11.ve_ref, ...), custom_call_target="tpu_custom_call" | custom-call | tf_op jit(solution)/shard_map/pallas_call | solution.py:415
  83.4 1.9 %copy.14 = bf16[512,512]{1,0:T(8,128)(2,1)} copy(bf16[512,512]{1,0:T(8,128)(2,1)} %get-tuple-element.4) | data formatting | bytes 1048576
  85.3 2.5 %copy.15 = bf16[1344,512]{1,0:T(8,128)(2,1)} copy(bf16[1344,512]{1,0:T(8,128)(2,1)} %get-tuple-element.5) | data formatting | bytes 2752512

commit v4 on v2

--- a/solution.py
+++ b/solution.py
@@ -80,10 +80,10 @@
     half = rows // 2
     mine = lax.rem(b, 2) * half
     weight_copies, pair_copies = [], []
-    for t in list(range(2, nh)) + [1]:
+    for t in list(range(nh - 1, 0, -1)):
         to = partner(h, t)
         for m, ref in enumerate((wk_ref, wv_ref)):
-            if t == 1:
+            if t < 3:
                 src, dst = ref.at[pl.ds(to * rows, rows), :], weights.at[t, m]
             else:
                 src = ref.at[pl.ds(to * rows + mine, half), :]
@@ -113,7 +113,7 @@
         at = slice(j * SCALE_BLOCK, (j + 1) * SCALE_BLOCK)
         for g in range(heads):
             key_true[at, cols(g)] = (
-                k_ref[at, cols(g)].astype(F32) * power_of_two(ke_ref[j, g])
+                k_ref[at, cols(g)].astype(F32) * power_of_two(ke_ref[j : j + 1, g : g + 1])
             ).astype(BF16)
     key_far = along(key_true, raw_far, fwd_send.at[0], fwd_recv.at[0], 2)
     when_start(b + 2 < n, [key_far])
@@ -127,7 +127,7 @@
         at = slice(j * SCALE_BLOCK, (j + 1) * SCALE_BLOCK)
         for g in range(heads):
             value[g, own + j * SCALE_BLOCK : own + (j + 1) * SCALE_BLOCK, :] = (
-                v_ref[at, cols(g)].astype(F32) * power_of_two(ve_ref[j, g])
+                v_ref[at, cols(g)].astype(F32) * power_of_two(ve_ref[j : j + 1, g : g + 1])
             ).astype(BF16)
 
     def halo(ref, g, kind):
@@ -218,6 +218,8 @@
             for copies in halos[g]:
                 copies[1].wait_recv()
 
+        if g == 0:
+            hand_over(0, len(pair_copies))
         smooth_t[...] = smooth[g].astype(F32).T.astype(BF16)
 
         def one_tile(i, carry, g=g):
@@ -259,8 +261,6 @@
         copy = along(grad_out.at[g, 0], grad_in.at[g, 0], g_send.at[g], g_recv.at[g], -1)
         when_start(b >= 1, [copy])
         near_copies.append(copy)
-        share = -(-len(pair_copies) // heads)
-        hand_over(g * share, (g + 1) * share)
 
     share_copies = []
     onward = []
@@ -291,7 +291,7 @@
                 whole = ref[g, here, :] * factor
                 for d in (1, 2):
                     whole = whole + grad_in[g, d - 1, at, cols(m)].astype(F32)
-                scaled[g, at, cols(m)] = (whole * power_of_two(exponent[j, g])).astype(BF16)
+                scaled[g, at, cols(m)] = (whole * power_of_two(exponent[j : j + 1, g : g + 1])).astype(BF16)
         for t in list(range(2, nh, 2)) + [1]:
             copy = across(
                 scaled.at[g], gathered.at[t - 1, g], s_send.at[t - 1, g], s_recv.at[t - 1, g], t
@@ -324,13 +324,14 @@
     for copy in own_copies:
         copy.wait()
     for t in range(nh):
-        if t == 2:
+        if t == 3:
             for copy in pair_copies:
                 copy.wait_recv()
+        if t in (1, 2):
+            for source, copy in weight_copies:
+                if source == t:
+                    copy.wait_recv()
         if t == 1:
-            for source, copy in weight_copies:
-                if source == 1:
-                    copy.wait_recv()
             for source, copy in share_copies:
                 if source == 1:
                     copy.wait_recv()
@@ -396,7 +397,6 @@
         assert ATTEND_WINDOW == 2 * tokens
         rows = wk.shape[0] // nh
         vmem = pl.BlockSpec(memory_space=pltpu.VMEM)
-        smem = pl.BlockSpec(memory_space=pltpu.SMEM)
         hbm = pl.BlockSpec(memory_space=pl.ANY)
         dma = pltpu.SemaphoreType.DMA
         return pl.pallas_call(
@@ -405,7 +405,7 @@
                 jax.ShapeDtypeStruct(q.shape, BF16),
                 jax.ShapeDtypeStruct((rows, tokens), BF16),
             ),
-            in_specs=[vmem, vmem, vmem, vmem, smem, smem, hbm, hbm],
+            in_specs=[vmem, vmem, vmem, vmem, vmem, vmem, hbm, hbm],
             out_specs=(vmem, vmem),
             scratch_shapes=[
                 pltpu.VMEM((tokens, width), BF16),

time: 86.6 us -> 78 us (0.901)
  the two profiles are of different devices: /device:TPU:9 before, /device:TPU:0 now
where the time goes in v4:
time: 78 us; the launch traced here: 77.8 us
  Pallas kernels  70.1 us (90%)
  local copies, waits for them, and re-layouts  7.04 us (9%)
    pallas_call x1, Pallas kernels, local(): pl.pallas_call(functools.partial(kernel, n, nh), out_shape=(jax.ShapeDtyp...  70.1 us
    unnamed x4, local copies, waits for them, and re-layouts  7.04 us

profile of v4, /device:TPU:0, one launch (start us, length us, event | category | flops | bytes accessed | tf_op | source)
XLA Modules:
  0.0 77.8 jit_solution(14035921767404260251)
XLA Ops:
  0.6 1.3 %copy.10.ke_ref = s32[4,2]{1,0:T(4,128)} copy(s32[4,2]{0,1:T(2,128)} %param.12) | data formatting | bytes 64 | tf_op args[4]
  2.0 1.3 %copy.11.ve_ref = s32[4,2]{1,0:T(4,128)} copy(s32[4,2]{0,1:T(2,128)} %param.13) | data formatting | bytes 64 | tf_op args[5]
  3.3 70.1 %shard_map.95 = (bf16[512,512]{1,0:T(8,128)(2,1)}, bf16[1344,512]{1,0:T(8,128)(2,1)}) custom-call(bf16[512,512]{1,0:T(8,128)(2,1)} %q_ref.1, bf16[512,256]{1,0:T(8,128)(2,1)} %k_ref.1, bf16[512,256]{1,0:T(8,128)(2,1)} %v_ref.1, bf16[512,512]{1,0:T(8,128)(2,1)} %do_ref.1, s32[4,2]{1,0:T(4,128)} %copy.10.ke_ref, s32[4,2]{1,0:T(4,128)} %copy.11.ve_ref, ...), custom_call_target="tpu_custom_call" | custom-call | tf_op jit(solution)/shard_map/pallas_call | solution.py:402
  73.4 1.9 %copy.14 = bf16[512,512]{1,0:T(8,128)(2,1)} copy(bf16[512,512]{1,0:T(8,128)(2,1)} %get-tuple-element.4) | data formatting | bytes 1048576
  75.3 2.5 %copy.15 = bf16[1344,512]{1,0:T(8,128)(2,1)} copy(bf16[1344,512]{1,0:T(8,128)(2,1)} %get-tuple-element.5) | data formatting | bytes 2752512
